TPU v7x, 32 devices: a whole 2x2x4 slice. The times are simulated.
32 devices in a mesh: group: 2 (over core), replica: 16 (over z, y, x).
Axes of the slice: x: 2, y: 2, z: 4, core: 2. Of those that a mesh axis runs over, the one named last changes fastest.
Arguments:
- tokens: bfloat16 [32768, 1152], P(('group', 'replica')), may hold values from -6 to 6
- out_grad: bfloat16 [32768, 1152], P(('group', 'replica')), may hold values from -6 to 6
- ln1_gain: bfloat16 [1152], P('group'), may hold values from 0.5 to 1.5
- ln1_bias: bfloat16 [1152], P('group'), may hold values from -3 to 3
- q_weight: bfloat16 [1152, 1152], P('group'), may hold values from -0.1875 to 0.1875
- q_bias: bfloat16 [1152], P('group'), may hold values from -3 to 3
- k_weight: bfloat16 [1152, 1152], P('group'), may hold values from -0.1875 to 0.1875
- v_weight: bfloat16 [1152, 1152], P('group'), may hold values from -0.1875 to 0.1875
- v_bias: bfloat16 [1152], P('group'), may hold values from -3 to 3
- o_weight: bfloat16 [1152, 1152], P('group'), may hold values from -2 to 2
- o_bias: bfloat16 [1152], P('group'), may hold values from -3 to 3
- ln2_gain: bfloat16 [1152], P('group'), may hold values from 0.5 to 1.5
- ln2_bias: bfloat16 [1152], P('group'), may hold values from -3 to 3
- up_weight: bfloat16 [1152, 4304], P('group'), may hold values from -0.1875 to 0.1875
- up_bias: bfloat16 [4304], P('group'), may hold values from -3 to 3
- down_weight: bfloat16 [4304, 1152], P('group'), may hold values from -0.09375 to 0.09375
- down_bias: bfloat16 [1152], P('group'), may hold values from -3 to 3
Outputs:
- activations: bfloat16 [32768, 1152], P(('group', 'replica'))
- input_grad: bfloat16 [32768, 1152], P(('group', 'replica'))
- ln1_gain_grad: float32 [1152], P('group')
- ln1_bias_grad: float32 [1152], P('group')
- q_weight_grad: float32 [1152, 1152], P('group')
- q_bias_grad: float32 [1152], P('group')
- k_weight_grad: float32 [1152, 1152], P('group')
- v_weight_grad: float32 [1152, 1152], P('group')
- v_bias_grad: float32 [1152], P('group')
- o_weight_grad: float32 [1152, 1152], P('group')
- o_bias_grad: float32 [1152], P('group')
- ln2_gain_grad: float32 [1152], P('group')
- ln2_bias_grad: float32 [1152], P('group')
- up_weight_grad: float32 [1152, 4304], P('group')
- up_bias_grad: float32 [4304], P('group')
- down_weight_grad: float32 [4304, 1152], P('group')
- down_bias_grad: float32 [1152], P('group')
All inputs are finite; a program needn't handle non-finite values.
Results may differ from a plain program's by a relative error of at most 0.018.
Values may be sent and summed in bfloat16 or wider, within the bound.
A program may use at most 256 MiB of HBM per device.

v0:
```python
import functools

import jax
import jax.numpy as jnp
from jax import lax
from jax.experimental import pallas as pl
from jax.experimental.pallas import tpu as pltpu
from jax.sharding import PartitionSpec as P

HEADS = 16
PATCHES = 128


def layer_norm(values, gain, shift):
    center = values - jnp.mean(values, axis=-1, keepdims=True)
    spread = jnp.mean(center * center, axis=-1, keepdims=True)
    return center * lax.rsqrt(spread + 1e-06) * gain + shift


def gelu_tanh(values):
    return jax.nn.gelu(values, approximate=True)


def split_heads(rows):
    return rows.reshape(-1, PATCHES, HEADS, rows.shape[-1] // HEADS)


def head_logits(query, key_rows):
    factor = (query.shape[-1] // HEADS) ** (-0.5)
    query_h = split_heads(query)
    key_h = split_heads(key_rows)
    logits = (
        jnp.einsum("isha,itha->ihst", query_h, key_h, preferred_element_type=jnp.float32) * factor
    )
    return (logits, query_h, key_h, factor)


def attend(query, key_rows, value_rows):
    logits, query_h, key_h, factor = head_logits(query, key_rows)
    peak = jnp.max(logits, axis=-1, keepdims=True)
    log_total = peak + jnp.log(jnp.sum(jnp.exp(logits - peak), axis=-1, keepdims=True))
    weights_low = jnp.exp(logits - log_total).astype(jnp.bfloat16)
    mixed = jnp.einsum(
        "ihst,itha->isha", weights_low, split_heads(value_rows), preferred_element_type=jnp.float32
    )
    return (mixed.reshape(query.shape), log_total)


def attend_back(query, key_rows, value_rows, log_total, d_mixed):
    logits, query_h, key_h, factor = head_logits(query, key_rows)
    weights = jnp.exp(logits - log_total)
    weights_low = weights.astype(jnp.bfloat16)
    value_h = split_heads(value_rows)
    d_mix_h = split_heads(d_mixed)
    d_weights = jnp.einsum("isha,itha->ihst", d_mix_h, value_h, preferred_element_type=jnp.float32)
    d_logits = weights * (d_weights - jnp.sum(weights * d_weights, axis=-1, keepdims=True))
    d_low = d_logits.astype(jnp.bfloat16)
    d_query = (
        jnp.einsum("ihst,itha->isha", d_low, key_h, preferred_element_type=jnp.float32) * factor
    ).astype(jnp.bfloat16)
    d_key = (
        jnp.einsum("ihst,isha->itha", d_low, query_h, preferred_element_type=jnp.float32) * factor
    ).astype(jnp.bfloat16)
    d_value = jnp.einsum(
        "ihst,isha->itha", weights_low, d_mix_h, preferred_element_type=jnp.float32
    ).astype(jnp.bfloat16)
    return (d_query.reshape(query.shape), d_key.reshape(query.shape), d_value.reshape(query.shape))


def outer_rows(left, right):
    return jnp.einsum("ra,rb->ab", left, right, preferred_element_type=jnp.float32)


def back_rows(grads, weight):
    return jnp.einsum("rb,ab->ra", grads, weight, preferred_element_type=jnp.float32)


def column_sums(grads):
    return jnp.sum(grads.astype(jnp.float32), axis=0)


def shards(
    tokens,
    out_grad,
    ln1_gain,
    ln1_bias,
    q_weight,
    q_bias,
    k_weight,
    v_weight,
    v_bias,
    o_weight,
    o_bias,
    ln2_gain,
    ln2_bias,
    up_weight,
    up_bias,
    down_weight,
    down_bias,
):
    attn_full = tuple(lax.all_gather(v, "group", axis=0, tiled=True) for v in (
        ln1_gain, ln1_bias, q_weight, q_bias, k_weight, v_weight, v_bias, o_weight, o_bias,
    ))
    gain_one, shift_one, wq_full, bq_full, wk_full, wv_full, bv_full, wo_full, bo_full = attn_full
    input_f = tokens.astype(jnp.float32)
    gain_one_f = gain_one.astype(jnp.float32)
    shift_one_f = shift_one.astype(jnp.float32)
    normed1 = layer_norm(input_f, gain_one_f, shift_one_f).astype(jnp.bfloat16)
    query = (
        jnp.dot(normed1, wq_full, preferred_element_type=jnp.float32) + bq_full.astype(jnp.float32)
    ).astype(jnp.bfloat16)
    key_rows = jnp.dot(normed1, wk_full, preferred_element_type=jnp.float32).astype(jnp.bfloat16)
    value_rows = (
        jnp.dot(normed1, wv_full, preferred_element_type=jnp.float32) + bv_full.astype(jnp.float32)
    ).astype(jnp.bfloat16)
    mixed, log_total = attend(query, key_rows, value_rows)
    attn_in = mixed.astype(jnp.bfloat16)
    residual = (
        input_f
        + jnp.dot(attn_in, wo_full, preferred_element_type=jnp.float32)
        + bo_full.astype(jnp.float32)
    )
    mlp_full = tuple(lax.all_gather(v, "group", axis=0, tiled=True) for v in (
        ln2_gain, ln2_bias, up_weight, up_bias, down_weight, down_bias,
    ))
    gain_two, shift_two, wup_full, bup_full, wdown_full, bdown_full = mlp_full
    gain_two_f = gain_two.astype(jnp.float32)
    shift_two_f = shift_two.astype(jnp.float32)
    normed2 = layer_norm(residual, gain_two_f, shift_two_f).astype(jnp.bfloat16)
    pre_act = jnp.dot(normed2, wup_full, preferred_element_type=jnp.float32) + bup_full.astype(
        jnp.float32
    )
    hidden = gelu_tanh(pre_act).astype(jnp.bfloat16)
    output = (
        residual
        + jnp.dot(hidden, wdown_full, preferred_element_type=jnp.float32)
        + bdown_full.astype(jnp.float32)
    )
    mlp_back = tuple(lax.all_gather(v, "group", axis=0, tiled=True) for v in (
        ln2_gain, ln2_bias, up_weight, up_bias, down_weight, down_bias,
    ))
    wup_back = mlp_back[2]
    wdown_back = mlp_back[4]
    grad_out = out_grad.astype(jnp.float32)
    d_wdown = outer_rows(hidden, out_grad)
    d_bdown = column_sums(out_grad)
    d_hidden = back_rows(out_grad, wdown_back)
    unused_act, gelu_back = jax.vjp(gelu_tanh, pre_act)
    d_pre = gelu_back(d_hidden)[0].astype(jnp.bfloat16)
    d_wup = outer_rows(normed2, d_pre)
    d_bup = column_sums(d_pre)
    d_normed2 = back_rows(d_pre, wup_back)
    unused_two, norm_back_two = jax.vjp(layer_norm, residual, gain_two_f, shift_two_f)
    d_res_norm, d_gain_two, d_shift_two = norm_back_two(d_normed2)
    d_residual = grad_out + d_res_norm
    mlp_grads = tuple(
        lax.psum_scatter(v.astype(jnp.bfloat16), "group", scatter_dimension=0, tiled=True).astype(jnp.float32)
        for v in (d_gain_two, d_shift_two, d_wup, d_bup, d_wdown, d_bdown)
    )
    attn_back = tuple(lax.all_gather(v, "group", axis=0, tiled=True) for v in (
        ln1_gain, ln1_bias, q_weight, q_bias, k_weight, v_weight, v_bias, o_weight, o_bias,
    ))
    wq_back = attn_back[2]
    wk_back = attn_back[4]
    wv_back = attn_back[5]
    wo_back = attn_back[7]
    d_attn = d_residual.astype(jnp.bfloat16)
    d_wout = outer_rows(attn_in, d_attn)
    d_bout = column_sums(d_attn)
    d_mixed = back_rows(d_attn, wo_back).astype(jnp.bfloat16)
    d_query, d_key, d_value = attend_back(query, key_rows, value_rows, log_total, d_mixed)
    d_wquery = outer_rows(normed1, d_query)
    d_bquery = column_sums(d_query)
    d_wkey = outer_rows(normed1, d_key)
    d_wvalue = outer_rows(normed1, d_value)
    d_bvalue = column_sums(d_value)
    d_normed1 = (
        back_rows(d_query, wq_back) + back_rows(d_key, wk_back) + back_rows(d_value, wv_back)
    )
    unused_one, norm_back_one = jax.vjp(layer_norm, input_f, gain_one_f, shift_one_f)
    d_in_norm, d_gain_one, d_shift_one = norm_back_one(d_normed1)
    d_input = (d_residual + d_in_norm).astype(jnp.bfloat16)
    attn_grads = tuple(
        lax.psum_scatter(v.astype(jnp.bfloat16), "group", scatter_dimension=0, tiled=True).astype(jnp.float32)
        for v in (d_gain_one, d_shift_one, d_wquery, d_bquery, d_wkey, d_wvalue, d_bvalue, d_wout, d_bout)
    )
    summed = tuple(
        lax.psum(v.astype(jnp.bfloat16), "replica").astype(jnp.float32) for v in attn_grads + mlp_grads
    )
    attn_grads = tuple(summed[:9])
    mlp_grads = tuple(summed[9:])
    return (output.astype(jnp.bfloat16), d_input) + tuple(attn_grads) + tuple(mlp_grads)


MESH = pl.DeviceIdType.MESH
bf16 = jnp.bfloat16
f32 = jnp.float32
ANY = pl.BlockSpec(memory_space=pl.ANY)
WIDTH = 1152
HALF = 576
FF = 4304
FF_HALF = 2152
TILES = 17
TILE = 128
FF_PAD = 2 * TILES * TILE
FIRST = 320
SECOND = 256


class Place:
    def __init__(self):
        self.core = lax.axis_index("group")
        chip = lax.axis_index("replica")
        self.chip = chip
        self.x = lax.rem(chip, 2)
        self.y = lax.rem(chip // 2, 2)
        self.z = chip // 4
        self.x_pair = chip + 1 - 2 * self.x
        self.y_pair = chip + 2 - 4 * self.y
        self.z_pair = chip + 4 - 8 * lax.rem(self.z, 2)
        self.inner = (self.z == 1) | (self.z == 2)
        self.outer = jnp.logical_not(self.inner)
        self.mid_pair = jnp.where(self.inner, chip + 12 - 8 * self.z, chip)
        self.z_half = lax.rem(self.z // 2, 2)

    def barrier(self):
        sem = pltpu.get_barrier_semaphore()

        def greet(core, chip):
            pl.semaphore_signal(sem, inc=1, device_id=(core, chip), device_id_type=MESH)

        greet(1 - self.core, self.chip)
        greet(self.core, self.x_pair)
        greet(self.core, self.y_pair)
        greet(self.core, self.z_pair)

        @pl.when(self.inner)
        def _():
            greet(self.core, self.mid_pair)
            pl.semaphore_wait(sem, 5)

        @pl.when(self.outer)
        def _():
            pl.semaphore_wait(sem, 4)

    def copy(self, source, target, sent, got, chip):
        return pltpu.make_async_remote_copy(
            source, target, sent, got, device_id=(self.core, chip), device_id_type=MESH
        )

    def copy_sibling(self, source, target, sent, got):
        return pltpu.make_async_remote_copy(
            source, target, sent, got, device_id=(1 - self.core, self.chip), device_id_type=MESH
        )


def aligned(value, unit):
    return pl.multiple_of(value, unit)


def landing(slots, chunk):
    return slots.at[lax.rem(chunk, slots.shape[0])]


def add_rows(total, landed, chunk, start, count):
    rows = pl.ds(start, count)
    slot = lax.rem(chunk, total.shape[0])
    total[slot, rows, :] = total[slot, rows, :] + landed[...]


class TreeFirst:
    steps = 9
    after = 0

    def __init__(self, place, total, final, spot, landing, sent, got, kept):
        self.at = place
        self.total = total
        self.final = final
        self.spot = spot
        self.kept = kept
        self.land = landing
        self.sent = sent
        self.got = got
        n = total.shape[1]
        self.n = n
        p = place
        self.own = [
            (0, n),
            (aligned(p.z_half * (n // 2), n // 2), n // 2),
        ]
        self.other = [None, (aligned((1 - p.z_half) * (n // 2), n // 2), n // 2)]
        for bit, part in ((p.y, n // 4), (p.x, n // 8)):
            base = self.own[-1][0]
            self.own.append((aligned(base + bit * part, part), part))
            self.other.append((aligned(base + (1 - bit) * part, part), part))
        self.peer = [p.z_pair, p.mid_pair, p.y_pair, p.x_pair]

    def flags(self, k, chunk):
        slot = lax.rem(chunk + self.after, self.sent.shape[1])
        return self.sent.at[k, slot], self.got.at[k, slot]

    def rows(self, chunk, span):
        return landing(self.total, chunk).at[pl.ds(span[0], span[1]), :]

    def ends(self, chunk, span):
        return self.final.at[self.spot(chunk), pl.ds(span[0], span[1]), :]

    def send(self, k, chunk):
        sent, got = self.flags(k, chunk)
        if k < 4:
            span = self.own[0] if k == 0 else self.other[k]
            return self.at.copy(
                self.rows(chunk, span), landing(self.land[k], chunk), sent, got, self.peer[k]
            )
        level = 7 - k
        target = self.ends(chunk, self.own[level])
        source = self.rows(chunk, self.own[3]) if k == 4 else target
        return self.at.copy(source, target, sent, got, self.peer[level])

    def keep(self, chunk):
        return pltpu.make_async_copy(
            self.rows(chunk, self.own[3]), self.ends(chunk, self.own[3]), landing(self.kept, chunk)
        )

    def arrive(self, k, chunk):
        if k < 4:
            landed = landing(self.land[k], chunk)
        else:
            level = 7 - k
            landed = self.ends(chunk, self.own[0] if level == 0 else self.other[level])
        self.at.copy(landed, landed, *self.flags(k, chunk), self.at.z_pair).wait_recv()

    def step(self, k, chunk):
        at = self.at
        if k == 0:

            @pl.when(at.outer)
            def _():
                self.send(0, chunk).start()

        elif k <= 7:

            @pl.when(at.inner)
            def _():
                self.arrive(k - 1, chunk)
                if k <= 4:
                    add_rows(self.total, landing(self.land[k - 1], chunk), chunk, *self.own[k - 1])
                if k == 4:
                    self.keep(chunk).start()
                if k == 5:
                    self.keep(chunk).wait()
                self.send(k, chunk).start()

        else:

            @pl.when(at.inner)
            def _():
                for j in range(1, 8):
                    self.send(j, chunk).wait_send()

            @pl.when(at.outer)
            def _():
                self.arrive(7, chunk)
                self.send(0, chunk).wait_send()


class PlaneFirst:
    steps = 8

    def __init__(
        self, place, total, final, spot, base, n, x_first, landing, sent, got, kept, after=0
    ):
        self.at = place
        self.after = after
        self.total = total
        self.final = final
        self.spot = spot
        self.kept = kept
        self.land = landing
        self.sent = sent
        self.got = got
        p = place
        if x_first:
            one, two = (p.x, p.x_pair), (p.y, p.y_pair)
        else:
            one, two = (p.y, p.y_pair), (p.x, p.x_pair)
        self.peer_one, self.peer_two = one[1], two[1]
        start = aligned(base + one[0] * (n // 2), 16)
        self.half = (start, n // 2)
        self.half_other = (aligned(base + (1 - one[0]) * (n // 2), 16), n // 2)
        self.quarter = (aligned(start + two[0] * (n // 4), 16), n // 4)
        self.quarter_other = (aligned(start + (1 - two[0]) * (n // 4), 16), n // 4)

    def flags(self, k, chunk):
        slot = lax.rem(chunk + self.after, self.sent.shape[1])
        return self.sent.at[k, slot], self.got.at[k, slot]

    def rows(self, chunk, span):
        return landing(self.total, chunk).at[pl.ds(span[0], span[1]), :]

    def ends(self, chunk, span):
        return self.final.at[self.spot(chunk), pl.ds(span[0], span[1]), :]

    def keep(self, chunk):
        return pltpu.make_async_copy(
            self.rows(chunk, self.quarter), self.ends(chunk, self.quarter), landing(self.kept, chunk + self.after)
        )

    def send(self, k, chunk):
        at = self.at
        quarter = self.rows(chunk, self.quarter)
        quarter_end = self.ends(chunk, self.quarter)
        half_end = self.ends(chunk, self.half)
        source, target, peer = (
            (self.rows(chunk, self.half_other), landing(self.land[0], chunk), self.peer_one),
            (self.rows(chunk, self.quarter_other), landing(self.land[1], chunk), self.peer_two),
            (quarter, landing(self.land[2], chunk), at.z_pair),
            (quarter, landing(self.land[3], chunk), at.mid_pair),
            (quarter, quarter_end, at.z_pair),
            (quarter_end, quarter_end, self.peer_two),
            (half_end, half_end, self.peer_one),
        )[k]
        return at.copy(source, target, *self.flags(k, chunk), peer)

    def arrive(self, k, chunk):
        if k < 4:
            landed = landing(self.land[k], chunk)
        else:
            landed = self.ends(
                chunk, (self.quarter, self.quarter_other, self.half_other)[k - 4]
            )
        self.at.copy(landed, landed, *self.flags(k, chunk), self.at.z_pair).wait_recv()

    def step(self, k, chunk):
        at = self.at
        if k == 0:
            self.send(0, chunk).start()
        elif k == 1:
            self.arrive(0, chunk)
            add_rows(self.total, landing(self.land[0], chunk), chunk, *self.half)
            self.send(1, chunk).start()
        elif k == 2:
            self.arrive(1, chunk)
            add_rows(self.total, landing(self.land[1], chunk), chunk, *self.quarter)

            @pl.when(at.outer)
            def _():
                self.send(2, chunk).start()

        elif k == 3:

            @pl.when(at.inner)
            def _():
                self.arrive(2, chunk)
                add_rows(self.total, landing(self.land[2], chunk), chunk, *self.quarter)
                self.send(3, chunk).start()

        elif k == 4:

            @pl.when(at.inner)
            def _():
                self.arrive(3, chunk)
                self.send(3, chunk).wait_send()
                add_rows(self.total, landing(self.land[3], chunk), chunk, *self.quarter)
                self.send(4, chunk).start()
                self.keep(chunk).start()

        elif k == 5:

            @pl.when(at.inner)
            def _():
                self.keep(chunk).wait()

            @pl.when(at.outer)
            def _():
                self.arrive(4, chunk)

            self.send(5, chunk).start()
        elif k == 6:
            self.arrive(5, chunk)
            self.send(6, chunk).start()
        else:
            self.arrive(6, chunk)
            for j in (0, 1, 5, 6):
                self.send(j, chunk).wait_send()

            @pl.when(at.inner)
            def _():
                self.send(4, chunk).wait_send()

            @pl.when(at.outer)
            def _():
                self.send(2, chunk).wait_send()


def tree_scratch(n, width):
    return [
        pltpu.VMEM((slots, n // part, width), bf16)
        for slots, part in ((10, 1), (3, 2), (3, 4), (3, 8))
    ] + flag_scratch(8, 10)


def plane_scratch(n, width):
    return [
        pltpu.VMEM((slots, n // part, width), bf16)
        for slots, part in ((3, 2), (3, 4), (4, 4), (3, 4))
    ]


def flag_scratch(copies, slots):
    return [
        pltpu.SemaphoreType.DMA((copies, slots)),
        pltpu.SemaphoreType.DMA((copies, slots)),
        pltpu.SemaphoreType.DMA((slots,)),
    ]


def dot(left, right, contract):
    return lax.dot_general(left, right, (contract, ((), ())), preferred_element_type=f32)


NN = ((1,), (0,))
NT = ((1,), (1,))
TN = ((0,), (0,))


def gelu_and_slope(u):
    c = 0.7978845608028654
    square = u * u
    t = jnp.tanh(c * u * (1.0 + 0.044715 * square))
    half = 0.5 * (1.0 + t)
    slope = half + 0.5 * u * (1.0 - t * t) * (c * (1.0 + 3 * 0.044715 * square))
    return u * half, slope


VECTORS = 8
LANES = 640
SCALE = 72**-0.5
HEAD = 72


def head_window(h):
    return slice(h * HEAD // 128 * 128, ((h + 1) * HEAD + 127) // 128 * 128)


def only_head(rows, h):
    lane = lax.broadcasted_iota(jnp.int32, rows.shape, 1) + head_window(h).start
    return jnp.where((lane >= h * HEAD) & (lane < (h + 1) * HEAD), rows, jnp.zeros_like(rows))


class Lanes:
    def __init__(self):
        self.tiles = [None] * (WIDTH // 128)

    def add(self, h, window):
        first = head_window(h).start // 128
        for j in range(window.shape[1] // 128):
            part = window[:, j * 128 : (j + 1) * 128]
            old = self.tiles[first + j]
            self.tiles[first + j] = part if old is None else old + part

    def joined(self, scale=None):
        tiles = self.tiles if scale is None else [t * scale for t in self.tiles]
        return jnp.concatenate([t.astype(bf16) for t in tiles], axis=1)


def normalise(rows, gain, shift):
    center = rows - jnp.mean(rows, axis=-1, keepdims=True)
    spread = jnp.mean(center * center, axis=-1, keepdims=True)
    return center * lax.rsqrt(spread + 1e-06) * gain + shift


def forward_kernel(
    tokens_ref,
    wq_ref,
    wk_ref,
    wv_ref,
    wo_ref,
    up_ref,
    down_ref,
    pack_ref,
    bup_ref,
    h1_ref,
    q_ref,
    k_ref,
    v_ref,
    ao_ref,
    probs_ref,
    x2_ref,
    h2_ref,
    w_ref,
    wup_ref,
    wdown_ref,
    vec_ref,
    bups_ref,
    x,
    h1,
    q,
    k,
    v,
    ao,
    probs,
    x2,
    h2,
    w,
    up,
    up_wide,
    down,
    zeros,
    pack,
    vec,
    local,
    wsem,
    psem,
    sent,
    got,
    bsem,
):
    at = Place()
    core = at.core
    own = pl.ds(aligned(core * HALF, HALF), HALF)
    ff_own = pl.ds(aligned(core * TILES * TILE, TILE), FF_HALF)
    shards = (wq_ref, wk_ref, wv_ref, wo_ref)
    load_x = pltpu.make_async_copy(tokens_ref, x, local.at[0])
    load_x.start()
    load_w = [pltpu.make_async_copy(s, w.at[j, own, :], local.at[1 + j]) for j, s in enumerate(shards)]
    load_pack = pltpu.make_async_copy(pack_ref, pack.at[core], local.at[5])
    load_bup = pltpu.make_async_copy(bup_ref, bups_ref.at[core], local.at[6])
    load_up = pltpu.make_async_copy(up_ref, up, local.at[7])
    load_down = pltpu.make_async_copy(down_ref, down, local.at[8])
    keep_down = pltpu.make_async_copy(down, wdown_ref.at[ff_own, :], wsem.at[4])
    for load in (load_pack, *load_w, load_bup, load_up, load_down):
        load.start()
    zeros[...] = jnp.zeros_like(zeros)
    gap = TILES * TILE - FF_HALF
    blanks = [
        pltpu.make_async_copy(
            zeros, wdown_ref.at[pl.ds(h * TILES * TILE + FF_HALF, gap), :], local.at[9 + h]
        )
        for h in (0, 1)
    ]
    for blank in blanks:
        blank.start()

    bar = pltpu.get_barrier_semaphore()
    pl.semaphore_signal(bar, inc=1, device_id=(1 - core, at.chip), device_id_type=MESH)
    pl.semaphore_wait(bar, 1)

    def share(j, source, target):
        return at.copy_sibling(source, target, sent.at[j], got.at[j])

    give_w = [share(j, s, w.at[j, own, :]) for j, s in enumerate(shards)]
    give_pack = share(4, pack_ref, pack.at[core])
    give_bup = share(5, bup_ref, bups_ref.at[core])
    give_down = share(6, down_ref, wdown_ref.at[ff_own, :])
    give_up = share(7, up_wide, wup_ref.at[own, :])
    keep_up = pltpu.make_async_copy(up_wide, wup_ref.at[own, :], local.at[11])
    give_pack.start()
    for give in give_w:
        give.start()
    give_bup.start()
    give_down.start()

    load_pack.wait()
    give_pack.wait()
    vec[...] = jnp.concatenate([pack[0, :, :HALF], pack[1, :, :HALF]], axis=1)
    load_x.wait()
    rows_of = [pl.ds(b * 512, 512) for b in range(2)]

    def first_norm(b, carry):
        rows = pl.ds(aligned(b * 128, 128), 128)
        h1[rows, :] = normalise(x[rows, :].astype(f32), vec[0:1, :], vec[1:2, :]).astype(bf16)
        return carry

    lax.fori_loop(0, 8, first_norm, 0)
    keep = [pltpu.make_async_copy(h1, h1_ref, local.at[0])]
    keep[0].start()

    def project(j, target, bias):
        load_w[j].wait()
        give_w[j].wait()
        for rows in rows_of:
            y = dot(h1[rows, :], w[j], NN)
            if bias is not None:
                y = y + vec[bias : bias + 1, :]
            target[rows, :] = y.astype(bf16)

    project(0, q, 2)
    project(1, k, None)
    project(2, v, 3)
    for j, (s, d) in enumerate(((q, q_ref), (k, k_ref), (v, v_ref))):
        keep.append(pltpu.make_async_copy(s, d, local.at[12 + j]))
        keep[-1].start()

    load_down.wait()
    keep_down.start()
    load_up.wait()

    def widen(b, carry):
        rows = pl.ds(aligned(b * 64, 64), 64)
        row = up[rows, :]
        none = jnp.zeros((64, gap), bf16)
        up_wide[rows, :] = jnp.concatenate([row[:, :FF_HALF], none, row[:, FF_HALF:], none], axis=1)
        return carry

    lax.fori_loop(0, HALF // 64, widen, 0)
    keep_up.start()
    give_up.start()

    def keep_probs(i):
        slot = lax.rem(i, 2)
        return pltpu.make_async_copy(probs.at[slot], probs_ref.at[i], psem.at[slot])

    def attention(i, carry):
        rows = pl.ds(aligned(i * 128, 128), 128)
        slot = lax.rem(i, 2)

        @pl.when(i >= 2)
        def _():
            keep_probs(i - 2).wait()

        qi, ki, vi = q[rows, :], k[rows, :], v[rows, :]
        mixed = Lanes()
        held = []
        for h in range(HEADS):
            cols = head_window(h)
            logits = dot(only_head(ki[:, cols], h), qi[:, cols], NT) * SCALE
            e = jnp.exp(logits - jnp.max(logits, axis=0, keepdims=True))
            p = (e / jnp.sum(e, axis=0, keepdims=True)).astype(bf16)
            held.append(p)
            mixed.add(h, dot(p, only_head(vi[:, cols], h), TN))
        ao[rows, :] = mixed.joined()
        probs[slot] = jnp.concatenate(held, axis=1)
        keep_probs(i).start()
        return carry

    lax.fori_loop(0, 8, attention, 0)
    keep_ao = pltpu.make_async_copy(ao, ao_ref, local.at[15])
    keep_ao.start()

    load_w[3].wait()
    give_w[3].wait()
    keep_w = pltpu.make_async_copy(w, w_ref, wsem.at[0])
    keep_w.start()
    keep_vec = pltpu.make_async_copy(vec, vec_ref, wsem.at[1])
    keep_vec.start()
    for rows in rows_of:
        x2[rows, :] = x[rows, :].astype(f32) + dot(ao[rows, :], w[3], NN) + vec[4:5, :]

    def second_norm(b, carry):
        rows = pl.ds(aligned(b * 128, 128), 128)
        h2[rows, :] = normalise(x2[rows, :], vec[5:6, :], vec[6:7, :]).astype(bf16)
        return carry

    lax.fori_loop(0, 8, second_norm, 0)
    keep_x2 = pltpu.make_async_copy(x2, x2_ref, wsem.at[2])
    keep_h2 = pltpu.make_async_copy(h2, h2_ref, wsem.at[3])
    for copy in (keep_x2, keep_h2):
        copy.start()
    for copy in (
        *keep,
        keep_probs(6),
        keep_probs(7),
        keep_ao,
        keep_w,
        keep_vec,
        load_bup,
        keep_down,
        *blanks,
        keep_up,
        keep_x2,
        keep_h2,
    ):
        copy.wait()
    for give in (give_bup, give_down, give_up):
        give.wait()


def forward(tokens, wq, wk, wv, wo, up, down, pack, bup):
    rows = tokens.shape[0]
    images = rows // PATCHES
    flat = jax.ShapeDtypeStruct((rows, WIDTH), bf16)
    return pl.pallas_call(
        forward_kernel,
        out_shape=(
            flat,
            flat,
            flat,
            flat,
            flat,
            jax.ShapeDtypeStruct((images, PATCHES, HEADS * PATCHES), bf16),
            jax.ShapeDtypeStruct((rows, WIDTH), f32),
            flat,
            jax.ShapeDtypeStruct((4, WIDTH, WIDTH), bf16),
            jax.ShapeDtypeStruct((WIDTH, FF_PAD), bf16),
            jax.ShapeDtypeStruct((FF_PAD, WIDTH), bf16),
            jax.ShapeDtypeStruct((VECTORS, WIDTH), f32),
            jax.ShapeDtypeStruct((2, TILES, 1, TILE), f32),
        ),
        in_specs=[ANY] * 9,
        out_specs=[ANY] * 13,
        scratch_shapes=[pltpu.VMEM((rows, WIDTH), bf16)] * 6
        + [
            pltpu.VMEM((2, PATCHES, HEADS * PATCHES), bf16),
            pltpu.VMEM((rows, WIDTH), f32),
            pltpu.VMEM((rows, WIDTH), bf16),
            pltpu.VMEM((4, WIDTH, WIDTH), bf16),
            pltpu.VMEM((HALF, FF), bf16),
            pltpu.VMEM((HALF, FF_PAD), bf16),
            pltpu.VMEM((FF_HALF, WIDTH), bf16),
            pltpu.VMEM((TILES * TILE - FF_HALF, WIDTH), bf16),
            pltpu.VMEM((2, VECTORS, LANES), f32),
            pltpu.VMEM((VECTORS, WIDTH), f32),
            pltpu.SemaphoreType.DMA((16,)),
            pltpu.SemaphoreType.DMA((5,)),
            pltpu.SemaphoreType.DMA((2,)),
            pltpu.SemaphoreType.DMA((8,)),
            pltpu.SemaphoreType.DMA((8,)),
            pltpu.SemaphoreType.DMA((1,)),
        ],
        compiler_params=pltpu.CompilerParams(
            collective_id=3, has_side_effects=True, vmem_limit_bytes=62 * 2**20
        ),
        name="forward",
    )(tokens, wq, wk, wv, wo, up, down, pack, bup)


CHUNKS = 9
TREE = TILES + CHUNKS
SMALL = TILES + 2 * CHUNKS + 1
BLOCK = 128
FF_TICKS = 15
NORM_TICK = 4
VALUE_TICK = 3


def rest_kernel(
    tokens_ref,
    og_ref,
    h1_ref,
    q_ref,
    k_ref,
    v_ref,
    ao_ref,
    probs_ref,
    x2_ref,
    h2_ref,
    w_ref,
    wup_ref,
    wdown_ref,
    vec_ref,
    bup_ref,
    out_ref,
    din_ref,
    g1_ref,
    g2_ref,
    h2,
    h2t,
    og,
    dh2,
    bup,
    vec,
    dbup,
    dvec,
    small,
    sib1,
    sib2,
    sib3,
    sum1,
    sum2,
    sum3,
    local,
    gsent,
    ggot,
    *comm,
):
    at = Place()
    rows_all = h2.shape[0]
    blocks = rows_all // BLOCK
    flags = comm[7:10], comm[10:13]
    planes = [comm[j : j + 4] for j in range(13, 29, 4)]

    def tree_spot(chunk):
        late = chunk - TILES
        value_or_query = jnp.where(late < 5, 2 * late, CHUNKS + 2 * late - 9)
        return jnp.where(chunk < TILES, chunk, TILES + value_or_query)

    def late_spot(chunk):
        return TILES + jnp.where(chunk < 4, 2 * chunk + 1, CHUNKS + 2 * chunk - 8)

    tree = TreeFirst(at, sum1, g1_ref, tree_spot, comm[:4], *comm[4:7])
    early = [
        PlaneFirst(at, sum2, g2_ref, lambda c: c, base, n, j == 0, planes[j], *flags[j])
        for j, base, n in ((0, 0, FIRST), (1, FIRST, SECOND))
    ]
    late = [
        PlaneFirst(
            at, sum3, g1_ref, late_spot, base, TILE // 2, j == 0, planes[2 + j], *flags[j], TILES
        )
        for j, base in ((0, 0), (1, TILE // 2))
    ]

    def advance(tick):
        for k in reversed(range(TreeFirst.steps)):
            chunk = tick - k

            @pl.when((chunk >= 0) & (chunk < TREE))
            def _():
                tree.step(k, chunk)

            if k < PlaneFirst.steps:

                @pl.when((chunk >= 0) & (chunk < TILES))
                def _():
                    for part in early:
                        part.step(k, chunk)

                @pl.when((chunk >= TILES) & (chunk <= TREE))
                def _():
                    late[0].step(k, chunk - TILES)

                @pl.when((chunk >= TILES) & (chunk < TREE))
                def _():
                    late[1].step(k, chunk - TILES)

    def block(b):
        return pl.ds(aligned(b * BLOCK, BLOCK), BLOCK)

    loads = [
        pltpu.make_async_copy(s, d, local.at[j])
        for j, (s, d) in enumerate(
            ((h2_ref, h2), (og_ref, og), (bup_ref, bup), (vec_ref, vec))
        )
    ]
    for load in loads:
        load.start()
    dvec[...] = jnp.zeros_like(dvec)

    def feed_forward(out, staged, wu, wd, mine1, mine2, wsem):
        load_x2 = pltpu.make_async_copy(x2_ref, out, local.at[4])
        load_x2.start()

        def weights(i, slot):
            cols = [pl.ds(aligned(h * TILES * TILE + i * TILE, TILE), TILE) for h in (0, 1)]
            parts = []
            for h in (0, 1):
                here = pl.ds(h * TILE, TILE)
                parts.append(
                    pltpu.make_async_copy(
                        wup_ref.at[:, cols[h]], wu.at[slot, :, here], wsem.at[h, slot]
                    )
                )
                parts.append(
                    pltpu.make_async_copy(
                        wdown_ref.at[cols[h], :], wd.at[slot, here, :], wsem.at[2 + h, slot]
                    )
                )
            return parts

        for part in weights(0, 0):
            part.start()
        at.barrier()
        for load in loads:
            load.wait()
        load_x2.wait()
        for b in range(blocks):
            rows = pl.ds(b * BLOCK, BLOCK)
            h2t[:, rows] = h2[rows, :].T
        out[...] = out[...] + vec[7:8, :]
        dh2[...] = jnp.zeros_like(dh2)

        def to_sibling(slot):
            return [
                at.copy_sibling(m.at[slot, 1 - at.core], s.at[slot], gsent.at[j, slot], ggot.at[j, slot])
                for j, (m, s) in enumerate(((mine1, sib1), (mine2, sib2)))
            ]

        def meet(i):
            slot = lax.rem(i, 2)
            for copy in to_sibling(slot):
                copy.wait()
            sum1[i] = mine1[slot, at.core] + sib1[slot]
            sum2[i] = mine2[slot, at.core] + sib2[slot]

        def tile(i, carry):
            slot = lax.rem(i, 2)

            @pl.when(i >= 1)
            def _():
                meet(i - 1)

            turn = i * FF_TICKS // (TILES - 1)

            @pl.when(turn > (i - 1) * FF_TICKS // (TILES - 1))
            def _():
                advance(turn - 1)

            for part in weights(i, slot):
                part.wait()

            @pl.when(i + 1 < TILES)
            def _():
                for part in weights(i + 1, 1 - slot):
                    part.start()

            bias = jnp.concatenate([bup[0, i], bup[1, i]], axis=1)
            u = dot(h2[...], wu[slot], NN) + bias
            a, slope = gelu_and_slope(u)
            a = a.astype(bf16)
            out[...] += dot(a, wd[slot], NN)
            d_wd = dot(a, og[...], TN).astype(bf16)
            mine1[slot, 0] = d_wd[:TILE]
            mine1[slot, 1] = d_wd[TILE:]
            du = (dot(og[...], wd[slot], NT) * slope).astype(bf16)
            d_wu = dot(h2t[...], du, NN).astype(bf16)
            mine2[slot, 0] = d_wu[:HALF]
            mine2[slot, 1] = d_wu[HALF:]
            for copy in to_sibling(slot):
                copy.start()
            dh2[...] += dot(du, wu[slot], NT)
            dbup[i] = jnp.sum(du.astype(f32), axis=0, keepdims=True)
            return carry

        lax.fori_loop(0, TILES, tile, 0)
        meet(TILES - 1)

        def put(b):
            slot = lax.rem(b, 2)
            return pltpu.make_async_copy(staged.at[slot], out_ref.at[block(b), :], local.at[slot])

        def put_rows(b, carry):
            @pl.when(b >= 2)
            def _():
                put(b - 2).wait()

            staged[lax.rem(b, 2)] = out[block(b), :].astype(bf16)
            put(b).start()
            return carry

        lax.fori_loop(0, blocks, put_rows, 0)
        put(blocks - 2).wait()
        put(blocks - 1).wait()

    pl.run_scoped(
        feed_forward,
        pltpu.VMEM((rows_all, WIDTH), f32),
        pltpu.VMEM((2, BLOCK, WIDTH), bf16),
        pltpu.VMEM((2, WIDTH, 2 * TILE), bf16),
        pltpu.VMEM((2, 2 * TILE, WIDTH), bf16),
        pltpu.VMEM((2, 2, TILE, WIDTH), bf16),
        pltpu.VMEM((2, 2, HALF, 2 * TILE), bf16),
        pltpu.SemaphoreType.DMA((4, 2)),
    )

    def attention(aot, dq, dk, dv, w, image, pimage, wide, source, staged, mine3, wsem, isem):
        load_ao = pltpu.make_async_copy(ao_ref, dq, wsem.at[0])
        load_h1 = pltpu.make_async_copy(h1_ref, dk, wsem.at[1])

        def load_w(j, slot):
            return pltpu.make_async_copy(w_ref.at[j], w.at[slot], wsem.at[2 + slot])

        def load_x2(b):
            slot = lax.rem(b, 2)
            return pltpu.make_async_copy(x2_ref.at[block(b), :], wide.at[slot], isem.at[4, slot])

        def load_x(b):
            slot = lax.rem(b, 2)
            return pltpu.make_async_copy(
                tokens_ref.at[pair(b), :], source.at[slot], isem.at[0, slot]
            )

        def put(b):
            slot = lax.rem(b, 2)
            return pltpu.make_async_copy(staged.at[slot], din_ref.at[pair(b), :], isem.at[4, slot])

        def pair(b):
            return pl.ds(aligned(b * 2 * BLOCK, 2 * BLOCK), 2 * BLOCK)

        def load_probs(i):
            slot = lax.rem(i, 2)
            return pltpu.make_async_copy(probs_ref.at[i], pimage.at[slot], isem.at[3, slot])

        def load_image(i):
            slot = lax.rem(i, 2)
            return [
                pltpu.make_async_copy(s.at[block(i), :], image.at[j, slot], isem.at[j, slot])
                for j, s in enumerate((q_ref, k_ref, v_ref))
            ] + [load_probs(i)]

        load_x2(0).start()
        load_w(3, 0).start()
        load_ao.start()
        load_h1.start()
        load_w(1, 1).start()
        load_w(2, 2).start()
        load_probs(0).start()

        def column_sum(j, value):
            dvec[j : j + 1, :] += jnp.sum(value, axis=0, keepdims=True)

        def norm_back(source, gain, incoming):
            center = source - jnp.mean(source, axis=-1, keepdims=True)
            rate = lax.rsqrt(jnp.mean(center * center, axis=-1, keepdims=True) + 1e-06)
            n = center * rate
            scaled = incoming * gain
            first = jnp.mean(scaled, axis=-1, keepdims=True)
            second = jnp.mean(scaled * n, axis=-1, keepdims=True)
            return n, (scaled - first - n * second) * rate

        def second_norm(b, carry):
            @pl.when(b == NORM_TICK)
            def _():
                advance(FF_TICKS)

            load_x2(b).wait()

            @pl.when(b + 1 < blocks)
            def _():
                load_x2(b + 1).start()

            rows = block(b)
            e = dh2[rows, :]
            n, dn = norm_back(wide[lax.rem(b, 2)], vec[5:6, :], e)
            g = og[rows, :].astype(f32)
            dx2 = g + dn
            dt = dx2.astype(bf16)
            dh2[rows, :] = dx2
            h2[rows, :] = dt
            column_sum(5, e * n)
            column_sum(6, e)
            column_sum(7, g)
            column_sum(4, dt.astype(f32))
            return carry

        lax.fori_loop(0, blocks, second_norm, 0)
        load_ao.wait()
        load_h1.wait()
        for b in range(blocks):
            rows = pl.ds(b * BLOCK, BLOCK)
            aot[:, rows] = dq[rows, :].T
            h2t[:, rows] = dk[rows, :].T
        load_w(3, 0).wait()
        for b in range(2):
            rows = pl.ds(b * (rows_all // 2), rows_all // 2)
            og[rows, :] = dot(h2[rows, :], w[0], NT).astype(bf16)
        load_w(0, 0).start()

        def values(i, carry):
            @pl.when(i == VALUE_TICK)
            def _():
                advance(FF_TICKS + 1)

            slot = lax.rem(i, 2)
            load_probs(i).wait()

            @pl.when(i + 1 < blocks)
            def _():
                load_probs(i + 1).start()

            rows = block(i)
            gi = og[rows, :]
            total = Lanes()
            for h in range(HEADS):
                low = pimage[slot, :, h * PATCHES : (h + 1) * PATCHES]
                total.add(h, dot(low, only_head(gi[:, head_window(h)], h), NN))
            dvi = total.joined()
            dv[rows, :] = dvi
            column_sum(3, dvi.astype(f32))
            return carry

        lax.fori_loop(0, blocks, values, 0)
        for copy in load_image(0):
            copy.start()

        def to_sibling(slot):
            return [
                at.copy_sibling(
                    mine3.at[slot, j, 1 - at.core],
                    sib3.at[slot, j],
                    gsent.at[2 + j, slot],
                    ggot.at[2 + j, slot],
                )
                for j in (0, 1)
            ]

        def meet(i):
            slot = lax.rem(i, 2)
            for copy in to_sibling(slot):
                copy.wait()
            for j, (s, c) in enumerate(((sum1, i + TILES), (sum3, i))):
                c = lax.rem(c, s.shape[0])
                s[c] = mine3[slot, j, at.core] + sib3[slot, j]

        def weight_rows(left, right, start, count):
            rows = [left[pl.ds(aligned(h * HALF + start, 64), count), :] for h in (0, 1)]
            return dot(jnp.concatenate(rows, axis=0), right[...], NN).astype(bf16)

        def produce(m, start, one, two):
            slot = lax.rem(m, 2)
            one = weight_rows(*one, start, TILE)
            two = weight_rows(*two, start, TILE)
            for h in (0, 1):
                for j in (0, 1):
                    part = slice(h * TILE + j * 64, h * TILE + j * 64 + 64)
                    mine3[slot, j, h] = jnp.concatenate([one[part], two[part]], axis=0)
            for copy in to_sibling(slot):
                copy.start()

        def heads(i, carry):
            @pl.when(lax.rem(i, 2) == 0)
            def _():
                produce(i // 2, i * 64, (h2t, dv), (aot, h2))

            slot = lax.rem(i, 2)
            for copy in load_image(i):
                copy.wait()

            @pl.when(i + 1 < blocks)
            def _():
                for copy in load_image(i + 1):
                    copy.start()

            @pl.when(lax.rem(i, 2) == 1)
            def _():
                meet(i // 2)
                advance(TILES + i // 2)

            rows = block(i)
            qi, ki, vi, gi = image[0, slot], image[1, slot], image[2, slot], og[rows, :]
            sums = Lanes(), Lanes()
            for h in range(HEADS):
                cols = head_window(h)
                p = pimage[slot, :, h * PATCHES : (h + 1) * PATCHES].astype(f32)
                dp = dot(only_head(vi[:, cols], h), gi[:, cols], NT)
                ds = (p * (dp - jnp.sum(p * dp, axis=0, keepdims=True))).astype(bf16)
                sums[0].add(h, dot(ds, only_head(ki[:, cols], h), TN))
                sums[1].add(h, dot(ds, only_head(qi[:, cols], h), NN))
            dqi, dki = sums[0].joined(SCALE), sums[1].joined(SCALE)
            dq[rows, :] = dqi
            dk[rows, :] = dki
            column_sum(2, dqi.astype(f32))
            return carry

        lax.fori_loop(0, blocks, heads, 0)
        for j in range(3):
            load_w(j, j).wait()
        load_x(0).start()

        vo = weight_rows(h2t, dv, 512, 64), weight_rows(aot, h2, 512, 64)
        qk = weight_rows(h2t, dq, 0, 64), weight_rows(h2t, dk, 0, 64)
        for h in (0, 1):
            part = slice(h * 64, h * 64 + 64)
            for j, (one, two) in enumerate((vo, qk)):
                mine3[0, j, h] = jnp.concatenate([one[part], two[part]], axis=0)
        for copy in to_sibling(0):
            copy.start()

        def weight_gradients(j, carry):
            meet(j - 1)

            @pl.when(j < CHUNKS)
            def _():
                produce(j, (j - 5) * TILE + 64, (h2t, dq), (h2t, dk))

            advance(TILES - 1 + j)

            @pl.when(j < CHUNKS)
            def _():
                b = j - 5
                load_x(b).wait()

                @pl.when(b + 1 < 4)
                def _():
                    load_x(b + 1).start()

                @pl.when(b >= 2)
                def _():
                    put(b - 2).wait()

                rows = pair(b)
                e = dot(dq[rows, :], w[0], NT) + dot(dk[rows, :], w[1], NT)
                e = e + dot(dv[rows, :], w[2], NT)
                x = source[lax.rem(b, 2)].astype(f32)
                n, dn = norm_back(x, vec[0:1, :], e)
                staged[lax.rem(b, 2)] = (dh2[rows, :] + dn).astype(bf16)
                put(b).start()
                column_sum(0, e * n)
                column_sum(1, e)

            return carry

        lax.fori_loop(5, CHUNKS + 1, weight_gradients, 0)
        put(2).wait()
        put(3).wait()

        small[...] = jnp.zeros_like(small)
        small[0:VECTORS, :] = dvec[...]
        for i in range(TILES):
            small[VECTORS + i : VECTORS + i + 1, : 2 * TILE] = dbup[i]
        mine3[1, 1, 0] = jnp.concatenate(
            [small[...].astype(bf16), jnp.zeros((TILE - small.shape[0], WIDTH), bf16)], axis=0
        )
        trade = at.copy_sibling(mine3.at[1, 1, 0], sib3.at[1, 1], gsent.at[3, 1], ggot.at[3, 1])
        trade.start()
        trade.wait()
        sum3[CHUNKS] = mine3[1, 1, 0] + sib3[1, 1]

    flat = pltpu.VMEM((rows_all, WIDTH), bf16)
    pl.run_scoped(
        attention,
        pltpu.VMEM((WIDTH, rows_all), bf16),
        flat,
        flat,
        flat,
        pltpu.VMEM((3, WIDTH, WIDTH), bf16),
        pltpu.VMEM((3, 2, BLOCK, WIDTH), bf16),
        pltpu.VMEM((2, PATCHES, HEADS * PATCHES), bf16),
        pltpu.VMEM((2, BLOCK, WIDTH), f32),
        pltpu.VMEM((2, 2 * BLOCK, WIDTH), bf16),
        pltpu.VMEM((2, 2 * BLOCK, WIDTH), bf16),
        pltpu.VMEM((2, 2, 2, TILE, WIDTH), bf16),
        pltpu.SemaphoreType.DMA((5,)),
        pltpu.SemaphoreType.DMA((5, 2)),
    )

    def drain(tick, carry):
        advance(tick)
        return carry

    lax.fori_loop(TREE, TREE + 8, drain, 0)


def rest_of_layer(tokens, og, h1, q, k, v, ao, probs, x2, h2, w, wup, wdown, vec, bup):
    rows = h2.shape[0]
    flat = jax.ShapeDtypeStruct((rows, WIDTH), bf16)
    return pl.pallas_call(
        rest_kernel,
        out_shape=(
            flat,
            flat,
            jax.ShapeDtypeStruct((SMALL + 1, TILE, WIDTH), bf16),
            jax.ShapeDtypeStruct((TILES, HALF, 2 * TILE), bf16),
        ),
        in_specs=[ANY] * 15,
        out_specs=[ANY] * 4,
        scratch_shapes=[
            pltpu.VMEM((rows, WIDTH), bf16),
            pltpu.VMEM((WIDTH, rows), bf16),
            pltpu.VMEM((rows, WIDTH), bf16),
            pltpu.VMEM((rows, WIDTH), f32),
            pltpu.VMEM((2, TILES, 1, TILE), f32),
            pltpu.VMEM((VECTORS, WIDTH), f32),
            pltpu.VMEM((TILES, 1, 2 * TILE), f32),
            pltpu.VMEM((VECTORS, WIDTH), f32),
            pltpu.VMEM((32, WIDTH), f32),
            pltpu.VMEM((2, TILE, WIDTH), bf16),
            pltpu.VMEM((2, HALF, 2 * TILE), bf16),
            pltpu.VMEM((2, 2, TILE, WIDTH), bf16),
            pltpu.VMEM((TILES + 1, TILE, WIDTH), bf16),
            pltpu.VMEM((TILES, HALF, 2 * TILE), bf16),
            pltpu.VMEM((CHUNKS + 1, TILE, WIDTH), bf16),
            pltpu.SemaphoreType.DMA((5,)),
            pltpu.SemaphoreType.DMA((4, 2)),
            pltpu.SemaphoreType.DMA((4, 2)),
        ]
        + tree_scratch(TILE, WIDTH)
        + flag_scratch(7, 8) * 2
        + plane_scratch(FIRST, 2 * TILE)
        + plane_scratch(SECOND, 2 * TILE)
        + plane_scratch(TILE // 2, WIDTH) * 2,
        compiler_params=pltpu.CompilerParams(
            collective_id=1, has_side_effects=True, vmem_limit_bytes=62 * 2**20
        ),
        name="rest_of_layer",
    )(tokens, og, h1, q, k, v, ao, probs, x2, h2, w, wup, wdown, vec, bup)


def finish_kernel(
    g1_ref, q_ref, k_ref, g2_ref, v_ref, o_ref, d1_ref, d2_ref, dq_ref, dk_ref, dv_ref, do_ref
):
    d1_ref[...] = g1_ref[0].astype(f32)
    parts = []
    for h in (0, 1):
        for i in range(TILES):
            wide = TILE if i < TILES - 1 else FF_HALF - (TILES - 1) * TILE
            parts.append(g2_ref[i, :, h * TILE : h * TILE + wide].astype(f32))
    d2_ref[...] = jnp.concatenate(parts, axis=1)
    for s, d in ((q_ref, dq_ref), (k_ref, dk_ref), (v_ref, dv_ref), (o_ref, do_ref)):
        d[...] = s[0].astype(f32)


def finish(g1, g2):
    steps = HALF // 32
    square = jax.ShapeDtypeStruct((HALF, WIDTH), f32)
    last = TILES - 1

    def quarter(first, offset):
        return pl.BlockSpec((1, 32, WIDTH), lambda i: (first + i // 2, offset + i % 2, 0))

    return pl.pallas_call(
        finish_kernel,
        grid=(steps,),
        out_shape=(
            jax.ShapeDtypeStruct((FF_HALF, WIDTH), f32),
            jax.ShapeDtypeStruct((HALF, FF), f32),
        )
        + (square,) * 4,
        in_specs=[
            pl.BlockSpec((1, TILE, WIDTH), lambda i: (jnp.minimum(i, last), 0, 0)),
            quarter(TREE, 0),
            quarter(TREE, 2),
            pl.BlockSpec((TILES, 32, 2 * TILE), lambda i: (0, i, 0)),
            quarter(TILES, 0),
            quarter(TILES, 2),
        ],
        out_specs=[
            pl.BlockSpec((TILE, WIDTH), lambda i: (jnp.minimum(i, last), 0)),
            pl.BlockSpec((32, FF), lambda i: (i, 0)),
        ]
        + [pl.BlockSpec((32, WIDTH), lambda i: (i, 0))] * 4,
        compiler_params=pltpu.CompilerParams(vmem_limit_bytes=62 * 2**20),
        name="finish",
    )(g1, g1, g1, g2, g1, g1)


def stack_kernel(*refs):
    rows = [r[...].astype(f32).reshape(1, HALF) for r in refs[:-1]]
    rows = jnp.concatenate(rows, axis=0)
    refs[-1][...] = jnp.concatenate([rows, jnp.zeros((VECTORS, LANES - HALF), f32)], axis=1)


def fast_shards(
    tokens,
    out_grad,
    ln1_gain,
    ln1_bias,
    q_weight,
    q_bias,
    k_weight,
    v_weight,
    v_bias,
    o_weight,
    o_bias,
    ln2_gain,
    ln2_bias,
    up_weight,
    up_bias,
    down_weight,
    down_bias,
):
    small = [ln1_gain, ln1_bias, q_bias, v_bias, o_bias, ln2_gain, ln2_bias, down_bias]
    pack = pl.pallas_call(
        stack_kernel, out_shape=jax.ShapeDtypeStruct((VECTORS, LANES), f32), name="stack"
    )(*small)
    gap = TILES * TILE - FF_HALF
    bup = jnp.pad(up_bias.astype(f32), (0, gap)).reshape(TILES, 1, TILE)
    saved = forward(
        tokens, q_weight, k_weight, v_weight, o_weight, up_weight, down_weight, pack, bup
    )
    output, d_input, g1, g2 = rest_of_layer(tokens, out_grad, *saved)
    d_down, d_up, d_q, d_k, d_v, d_o = finish(g1, g2)
    core = lax.axis_index("group")
    vectors = lax.dynamic_slice(g1[SMALL, :VECTORS], (0, core * HALF), (VECTORS, HALF)).astype(f32)
    d_bup = lax.dynamic_slice(
        g1[SMALL, VECTORS : VECTORS + TILES], (0, core * TILE), (TILES, TILE)
    )
    d_bup = d_bup.reshape(TILES * TILE)[:FF_HALF].astype(f32)
    return (
        output,
        d_input,
        vectors[0],
        vectors[1],
        d_q,
        vectors[2],
        d_k,
        d_v,
        vectors[3],
        d_o,
        vectors[4],
        vectors[5],
        vectors[6],
        d_up,
        d_bup,
        d_down,
        vectors[7],
    )


def solution(mesh):
    placed = (
        P(("group", "replica"), None),
        P(("group", "replica"), None),
        P("group"),
        P("group"),
        P("group", None),
        P("group"),
        P("group", None),
        P("group", None),
        P("group"),
        P("group", None),
        P("group"),
        P("group"),
        P("group"),
        P("group", None),
        P("group"),
        P("group", None),
        P("group"),
    )
    fast = mesh.shape["group"] == 2 and mesh.shape["replica"] == 16
    return jax.shard_map(
        fast_shards if fast else shards,
        mesh=mesh,
        in_specs=placed,
        out_specs=(
            P(("group", "replica"), None),
            P(("group", "replica"), None),
            P("group"),
            P("group"),
            P("group", None),
            P("group"),
            P("group", None),
            P("group", None),
            P("group"),
            P("group", None),
            P("group"),
            P("group"),
            P("group"),
            P("group", None),
            P("group"),
            P("group", None),
            P("group"),
        ),
        check_vma=False,
    )
```

profile of v0, /device:TPU:0, one launch (start us, length us, event | category | flops | bytes accessed | tf_op | source)
XLA Modules:
  0.0 393.6 jit_solution(17947680634010497303)
XLA Ops:
  0.7 0.7 pad_convert_fusion
  1.4 0.6 reshape.66.bup_ref
  2.0 1.4 stack.1.pack_ref
  3.4 47.6 %forward.1 = (bf16[1024,1152]{1,0:T(8,128)(2,1)}, bf16[1024,1152]{1,0:T(8,128)(2,1)}, bf16[1024,1152]{1,0:T(8,128)(2,1)}, bf16[1024,1152]{1,0:T(8,128)(2,1)}, bf...) custom-call(bf16[1024,1152]{1,0:T(8,128)(2,1)} %tokens_ref.3, ...), custom_call_target="tpu_custom_call" | custom-call | tf_op jit(solution)/shard_map/forward/pallas_call | solution.py:783
  51.0 314.8 %rest_of_layer.1 = (bf16[1024,1152]{1,0:T(8,128)(2,1)}, bf16[1024,1152]{1,0:T(8,128)(2,1)}, bf16[37,128,1152]{2,1,0:T(8,128)(2,1)}, bf16[17,576,256]{2,1,0:T(8,128)(2,1)}) custom-call(bf16[1024,1152]{1,0:T(8,128)(2,1)} %tokens_ref.3, bf16[1024,1152]{1,0:T(8,128)(2,1)} %og_ref.1, bf16[1024,1152]{1,0:T(8,128)(2,1)} %get-tuple-element.40.h1_ref, ...), custom_call_target="tpu_custom_call" | custom-call | tf_op jit(solution)/shard_map/rest_of_layer/pallas_call | solution.py:1336
  365.8 20.1 %finish.1 = (f32[2152,1152]{1,0:T(8,128)}, f32[576,4304]{1,0:T(8,128)}, f32[576,1152]{1,0:T(8,128)}, f32[576,1152]{1,0:T(8,128)}, f32[576,1152]{1,0:T(8,128)}, /*index=5*/f32[576,1152]{1,0:T(8,128)}) custom-call(bf16[37,128,1152]{2,1,0:T(8,128)(2,1)} %get-tuple-element.55.g1_ref.q_ref.k_ref.v_ref.o_ref, ...), custom_call_target="tpu_custom_call" | custom-call | tf_op jit(solution)/shard_map/finish/pallas_call | solution.py:1400
  385.9 0.8 slice.49
  386.8 0.6 slice_convert_fusion
  387.4 0.7 slice.41
  388.1 0.1 dynamic-slice_convert_fusion
  388.2 0.7 slice_reduce_fusion
  388.8 0.0 copy-start
  388.8 3.4 copy.36
  392.2 0.0 copy-done
  392.2 1.4 copy.37
  (1 shorter events, 0.0 us)
Async XLA Ops:
  388.8 3.4 copy-start
where the time goes:
time: 395 us; the launch traced here: 394 us
  Pallas kernels  384 us (97%)
  local copies, waits for them, and re-layouts  7.62 us (2%)
    pallas_call x1, Pallas kernels, rest_of_layer(): pl.pallas_call(rest_kernel, out_shape=(flat, flat, jax.ShapeDtypeStruct((...  315 us
    pallas_call x1, Pallas kernels, forward(): pl.pallas_call(forward_kernel, out_shape=(flat, flat, flat, flat, flat, j...  47.6 us
    pallas_call x1, Pallas kernels, finish(): pl.pallas_call(finish_kernel, grid=(steps,), out_shape=(jax.ShapeDtypeStr...  20.1 us

commit v1 on v0

--- a/solution.py
+++ b/solution.py
@@ -734,29 +734,33 @@
         keep_probs(i).start()
         return carry
 
-    lax.fori_loop(0, 8, attention, 0)
-    keep_ao = pltpu.make_async_copy(ao, ao_ref, local.at[15])
-    keep_ao.start()
-
     load_w[3].wait()
     give_w[3].wait()
     keep_w = pltpu.make_async_copy(w, w_ref, wsem.at[0])
     keep_w.start()
     keep_vec = pltpu.make_async_copy(vec, vec_ref, wsem.at[1])
     keep_vec.start()
-    for rows in rows_of:
-        x2[rows, :] = x[rows, :].astype(f32) + dot(ao[rows, :], w[3], NN) + vec[4:5, :]
+    lax.fori_loop(0, 8, attention, 0)
+    keep_ao = pltpu.make_async_copy(ao, ao_ref, local.at[15])
+    keep_ao.start()
 
     def second_norm(b, carry):
         rows = pl.ds(aligned(b * 128, 128), 128)
         h2[rows, :] = normalise(x2[rows, :], vec[5:6, :], vec[6:7, :]).astype(bf16)
         return carry
 
-    lax.fori_loop(0, 8, second_norm, 0)
-    keep_x2 = pltpu.make_async_copy(x2, x2_ref, wsem.at[2])
-    keep_h2 = pltpu.make_async_copy(h2, h2_ref, wsem.at[3])
-    for copy in (keep_x2, keep_h2):
-        copy.start()
+    keep_rows = []
+    for b, rows in enumerate(rows_of):
+        x2[rows, :] = x[rows, :].astype(f32) + dot(ao[rows, :], w[3], NN) + vec[4:5, :]
+        keep_rows.append(
+            pltpu.make_async_copy(x2.at[rows, :], x2_ref.at[rows, :], wsem.at[2 + b])
+        )
+        keep_rows[-1].start()
+        lax.fori_loop(4 * b, 4 * b + 4, second_norm, 0)
+        keep_rows.append(
+            pltpu.make_async_copy(h2.at[rows, :], h2_ref.at[rows, :], wsem.at[5 + b])
+        )
+        keep_rows[-1].start()
     for copy in (
         *keep,
         keep_probs(6),
@@ -768,8 +772,7 @@
         keep_down,
         *blanks,
         keep_up,
-        keep_x2,
-        keep_h2,
+        *keep_rows,
     ):
         copy.wait()
     for give in (give_bup, give_down, give_up):
@@ -812,7 +815,7 @@
             pltpu.VMEM((2, VECTORS, LANES), f32),
             pltpu.VMEM((VECTORS, WIDTH), f32),
             pltpu.SemaphoreType.DMA((16,)),
-            pltpu.SemaphoreType.DMA((5,)),
+            pltpu.SemaphoreType.DMA((7,)),
             pltpu.SemaphoreType.DMA((2,)),
             pltpu.SemaphoreType.DMA((8,)),
             pltpu.SemaphoreType.DMA((8,)),
@@ -1376,9 +1379,24 @@
 
 
 def finish_kernel(
-    g1_ref, q_ref, k_ref, g2_ref, v_ref, o_ref, d1_ref, d2_ref, dq_ref, dk_ref, dv_ref, do_ref
+    g1_ref,
+    q_ref,
+    k_ref,
+    g2_ref,
+    v_ref,
+    o_ref,
+    out_ref,
+    din_ref,
+    d1_ref,
+    d2_ref,
+    dq_ref,
+    dk_ref,
+    dv_ref,
+    do_ref,
+    out_end,
+    din_end,
 ):
-    d1_ref[...] = g1_ref[0].astype(f32)
+    d1_ref[...] = g1_ref[...].reshape(2 * TILE, WIDTH).astype(f32)
     parts = []
     for h in (0, 1):
         for i in range(TILES):
@@ -1387,15 +1405,18 @@
     d2_ref[...] = jnp.concatenate(parts, axis=1)
     for s, d in ((q_ref, dq_ref), (k_ref, dk_ref), (v_ref, dv_ref), (o_ref, do_ref)):
         d[...] = s[0].astype(f32)
-
-
-def finish(g1, g2):
-    steps = HALF // 32
+    out_end[...] = out_ref[...]
+    din_end[...] = din_ref[...]
+
+
+def finish(g1, g2, output, d_input):
+    steps = HALF // 64
     square = jax.ShapeDtypeStruct((HALF, WIDTH), f32)
-    last = TILES - 1
-
-    def quarter(first, offset):
-        return pl.BlockSpec((1, 32, WIDTH), lambda i: (first + i // 2, offset + i % 2, 0))
+    blocks = output.shape[0] // BLOCK
+    flat = pl.BlockSpec((BLOCK, WIDTH), lambda i: (jnp.minimum(i, blocks - 1), 0))
+
+    def half_chunk(first, part):
+        return pl.BlockSpec((1, 64, WIDTH), lambda i: (first + i, part, 0))
 
     return pl.pallas_call(
         finish_kernel,
@@ -1404,23 +1425,27 @@
             jax.ShapeDtypeStruct((FF_HALF, WIDTH), f32),
             jax.ShapeDtypeStruct((HALF, FF), f32),
         )
-        + (square,) * 4,
+        + (square,) * 4
+        + (jax.ShapeDtypeStruct(output.shape, bf16),) * 2,
         in_specs=[
-            pl.BlockSpec((1, TILE, WIDTH), lambda i: (jnp.minimum(i, last), 0, 0)),
-            quarter(TREE, 0),
-            quarter(TREE, 2),
-            pl.BlockSpec((TILES, 32, 2 * TILE), lambda i: (0, i, 0)),
-            quarter(TILES, 0),
-            quarter(TILES, 2),
+            pl.BlockSpec((2, TILE, WIDTH), lambda i: (i, 0, 0)),
+            half_chunk(TREE, 0),
+            half_chunk(TREE, 1),
+            pl.BlockSpec((TILES, 64, 2 * TILE), lambda i: (0, i, 0)),
+            half_chunk(TILES, 0),
+            half_chunk(TILES, 1),
+            flat,
+            flat,
         ],
         out_specs=[
-            pl.BlockSpec((TILE, WIDTH), lambda i: (jnp.minimum(i, last), 0)),
-            pl.BlockSpec((32, FF), lambda i: (i, 0)),
+            pl.BlockSpec((2 * TILE, WIDTH), lambda i: (i, 0)),
+            pl.BlockSpec((64, FF), lambda i: (i, 0)),
         ]
-        + [pl.BlockSpec((32, WIDTH), lambda i: (i, 0))] * 4,
+        + [pl.BlockSpec((64, WIDTH), lambda i: (i, 0))] * 4
+        + [flat] * 2,
         compiler_params=pltpu.CompilerParams(vmem_limit_bytes=62 * 2**20),
         name="finish",
-    )(g1, g1, g1, g2, g1, g1)
+    )(g1, g1, g1, g2, g1, g1, output, d_input)
 
 
 def stack_kernel(*refs):
@@ -1458,7 +1483,7 @@
         tokens, q_weight, k_weight, v_weight, o_weight, up_weight, down_weight, pack, bup
     )
     output, d_input, g1, g2 = rest_of_layer(tokens, out_grad, *saved)
-    d_down, d_up, d_q, d_k, d_v, d_o = finish(g1, g2)
+    d_down, d_up, d_q, d_k, d_v, d_o, output, d_input = finish(g1, g2, output, d_input)
     core = lax.axis_index("group")
     vectors = lax.dynamic_slice(g1[SMALL, :VECTORS], (0, core * HALF), (VECTORS, HALF)).astype(f32)
     d_bup = lax.dynamic_slice(

time: 395 us -> 390 us (0.987)
  local copies, waits for them, and re-layouts: 7.62 us -> 2.81 us
    unnamed x4 -> x0, local copies, waits for them, and re-layouts: 4.81 us -> none
where the time goes in v1:
time: 390 us; the launch traced here: 389 us
  Pallas kernels  384 us (98%)
    pallas_call x1, Pallas kernels, rest_of_layer(): pl.pallas_call(rest_kernel, out_shape=(flat, flat, jax.ShapeDtypeStruct((...  315 us
    pallas_call x1, Pallas kernels, forward(): pl.pallas_call(forward_kernel, out_shape=(flat, flat, flat, flat, flat, j...  47.9 us
    pallas_call x1, Pallas kernels, finish(): pl.pallas_call(finish_kernel, grid=(steps,), out_shape=(jax.ShapeDtypeStr...  20 us

profile of v1, /device:TPU:0, one launch (start us, length us, event | category | flops | bytes accessed | tf_op | source)
XLA Modules:
  0.0 389.0 jit_solution(16705103607124952952)
XLA Ops:
  0.7 0.7 pad_convert_fusion
  1.4 0.6 reshape.66.bup_ref
  2.0 1.4 stack.1.pack_ref
  3.4 47.9 %forward.1 = (bf16[1024,1152]{1,0:T(8,128)(2,1)}, bf16[1024,1152]{1,0:T(8,128)(2,1)}, bf16[1024,1152]{1,0:T(8,128)(2,1)}, bf16[1024,1152]{1,0:T(8,128)(2,1)}, bf...) custom-call(bf16[1024,1152]{1,0:T(8,128)(2,1)} %tokens_ref.3, ...), custom_call_target="tpu_custom_call" | custom-call | tf_op jit(solution)/shard_map/forward/pallas_call | solution.py:786
  51.3 314.8 %rest_of_layer.1 = (bf16[1024,1152]{1,0:T(8,128)(2,1)}, bf16[1024,1152]{1,0:T(8,128)(2,1)}, bf16[37,128,1152]{2,1,0:T(8,128)(2,1)}, bf16[17,576,256]{2,1,0:T(8,128)(2,1)}) custom-call(bf16[1024,1152]{1,0:T(8,128)(2,1)} %tokens_ref.3, bf16[1024,1152]{1,0:T(8,128)(2,1)} %og_ref.1, bf16[1024,1152]{1,0:T(8,128)(2,1)} %get-tuple-element.42.h1_ref, ...), custom_call_target="tpu_custom_call" | custom-call | tf_op jit(solution)/shard_map/rest_of_layer/pallas_call | solution.py:1339
  366.1 20.0 %finish.1 = (f32[2152,1152]{1,0:T(8,128)}, f32[576,4304]{1,0:T(8,128)}, f32[576,1152]{1,0:T(8,128)}, f32[576,1152]{1,0:T(8,128)}, f32[576,1152]{1,0:T(8,128)}, /...) custom-call(bf16[37,128,1152]{2,1,0:T(8,128)(2,1)} %get-tuple-element.55.g1_ref.q_ref.k_ref.v_ref.o_ref, ...), custom_call_target="tpu_custom_call" | custom-call | tf_op jit(solution)/shard_map/finish/pallas_call | solution.py:1421
  386.1 0.8 slice.49
  387.0 0.6 slice_convert_fusion
  387.6 0.7 slice.41
  388.3 0.1 dynamic-slice_convert_fusion
  388.4 0.7 slice_reduce_fusion
  (1 shorter events, 0.0 us)

commit v2 on v1

--- a/solution.py
+++ b/solution.py
@@ -503,7 +503,7 @@
 def plane_scratch(n, width):
     return [
         pltpu.VMEM((slots, n // part, width), bf16)
-        for slots, part in ((3, 2), (3, 4), (4, 4), (3, 4))
+        for slots, part in ((4, 2), (3, 4), (4, 4), (3, 4))
     ]
 
 
@@ -904,27 +904,28 @@
     ]
 
     def advance(tick):
-        for k in reversed(range(TreeFirst.steps)):
+        for k, j in ((0, 0), (7, 6), (6, 5), (5, 4), (4, 3), (3, 2), (2, 1), (1, None), (8, 7)):
             chunk = tick - k
 
             @pl.when((chunk >= 0) & (chunk < TREE))
             def _():
                 tree.step(k, chunk)
 
-            if k < PlaneFirst.steps:
-
-                @pl.when((chunk >= 0) & (chunk < TILES))
+            if j is not None:
+                part = tick - j
+
+                @pl.when((part >= 0) & (part < TILES))
                 def _():
-                    for part in early:
-                        part.step(k, chunk)
-
-                @pl.when((chunk >= TILES) & (chunk <= TREE))
+                    early[0].step(j, part)
+                    early[1].step(j, part)
+
+                @pl.when((part >= TILES) & (part <= TREE))
                 def _():
-                    late[0].step(k, chunk - TILES)
-
-                @pl.when((chunk >= TILES) & (chunk < TREE))
+                    late[0].step(j, part - TILES)
+
+                @pl.when((part >= TILES) & (part < TREE))
                 def _():
-                    late[1].step(k, chunk - TILES)
+                    late[1].step(j, part - TILES)
 
     def block(b):
         return pl.ds(aligned(b * BLOCK, BLOCK), BLOCK)

time: 390 us -> 387 us (level)
  no operation moved by 1% of the time
where the time goes in v2:
time: 387 us; the launch traced here: 386 us
  Pallas kernels  381 us (98%)
    pallas_call x1, Pallas kernels, rest_of_layer(): pl.pallas_call(rest_kernel, out_shape=(flat, flat, jax.ShapeDtypeStruct((...  312 us
    pallas_call x1, Pallas kernels, forward(): pl.pallas_call(forward_kernel, out_shape=(flat, flat, flat, flat, flat, j...  47.9 us
    pallas_call x1, Pallas kernels, finish(): pl.pallas_call(finish_kernel, grid=(steps,), out_shape=(jax.ShapeDtypeStr...  20 us

profile of v2, /device:TPU:0, one launch (start us, length us, event | category | flops | bytes accessed | tf_op | source)
XLA Modules:
  0.0 386.3 jit_solution(1912469575678466702)
XLA Ops:
  0.7 0.7 pad_convert_fusion
  1.4 0.6 reshape.66.bup_ref
  2.0 1.4 stack.1.pack_ref
  3.4 47.9 %forward.1 = (bf16[1024,1152]{1,0:T(8,128)(2,1)}, bf16[1024,1152]{1,0:T(8,128)(2,1)}, bf16[1024,1152]{1,0:T(8,128)(2,1)}, bf16[1024,1152]{1,0:T(8,128)(2,1)}, bf...) custom-call(bf16[1024,1152]{1,0:T(8,128)(2,1)} %tokens_ref.3, ...), custom_call_target="tpu_custom_call" | custom-call | tf_op jit(solution)/shard_map/forward/pallas_call | solution.py:786
  51.3 312.0 %rest_of_layer.1 = (bf16[1024,1152]{1,0:T(8,128)(2,1)}, bf16[1024,1152]{1,0:T(8,128)(2,1)}, bf16[37,128,1152]{2,1,0:T(8,128)(2,1)}, bf16[17,576,256]{2,1,0:T(8,128)(2,1)}) custom-call(bf16[1024,1152]{1,0:T(8,128)(2,1)} %tokens_ref.3, bf16[1024,1152]{1,0:T(8,128)(2,1)} %og_ref.1, bf16[1024,1152]{1,0:T(8,128)(2,1)} %get-tuple-element.42.h1_ref, ...), custom_call_target="tpu_custom_call" | custom-call | tf_op jit(solution)/shard_map/rest_of_layer/pallas_call | solution.py:1340
  363.4 20.0 %finish.1 = (f32[2152,1152]{1,0:T(8,128)}, f32[576,4304]{1,0:T(8,128)}, f32[576,1152]{1,0:T(8,128)}, f32[576,1152]{1,0:T(8,128)}, f32[576,1152]{1,0:T(8,128)}, /...) custom-call(bf16[37,128,1152]{2,1,0:T(8,128)(2,1)} %get-tuple-element.55.g1_ref.q_ref.k_ref.v_ref.o_ref, ...), custom_call_target="tpu_custom_call" | custom-call | tf_op jit(solution)/shard_map/finish/pallas_call | solution.py:1422
  383.4 0.8 slice.49
  384.2 0.6 slice_convert_fusion
  384.8 0.7 slice.41
  385.5 0.1 dynamic-slice_convert_fusion
  385.6 0.7 slice_reduce_fusion
  (1 shorter events, 0.0 us)
